TPU v7x, 32 devices: a whole 2x2x4 slice. The times are simulated.
32 devices in a mesh: wave: 4 (over z), tile: 8 (over y, x, core).
Axes of the slice: x: 2, y: 2, z: 4, core: 2. Of those that a mesh axis runs over, the one named last changes fastest.
Arguments:
- spectral: bfloat16 [640, 2, 64, 1281], P('wave', None, 'tile'), may hold values from -0.083496094 to 0.083496094
- legendre: bfloat16 [640, 8, 1281], P('wave'), may hold values from -0.25 to 0.25
- pair_ids: int32 [640], replicated, may hold values from 0 to 639, each once
Outputs:
- spectral_out: bfloat16 [640, 2, 64, 1281], P('wave', None, 'tile')
Inputs may be any that keep to these rules, and one draw needn't show every extreme that they name: A permutation: each pair 0 to 639 appears once; slot s of spectral, legendre and spectral_out holds wavenumbers pair_ids[s] and 1279 - pair_ids[s].
All inputs are finite; a program needn't handle non-finite values.
Results may differ from a plain program's by a relative error of at most 0.0072.
Values may be sent and summed in bfloat16 or wider, within the bound.
A program may use at most 64 MiB of HBM per device.

v0:
```python
import functools
import math
import jax
import jax.numpy as jnp
from jax import lax
from jax.sharding import PartitionSpec as P

MW = 1280
HALF_LATS = 1280
PAIRS = 640
NPTS = 5156
LANES = 128
RADIX = 32
F32 = jnp.float32
BF16 = jnp.bfloat16


def cycle_lengths(pair_number, pair_total):
    polar_cycle = pair_number * (HALF_LATS // 2) // pair_total
    cycle_index = jnp.stack([polar_cycle, HALF_LATS - 1 - polar_cycle])
    return (cycle_index, 20 + 4 * cycle_index)


def cycle_scale(cycle_index, cycle_len, lat_count):
    angles = math.pi * (cycle_index.astype(F32) + 0.5) / (2.0 * HALF_LATS)
    return 40.0 * jnp.sin(angles) / jnp.sqrt(lat_count * cycle_len.astype(F32))


def trig(wavenumbers, local_index, length):
    phase = wavenumbers[:, None] * local_index[None, :] % length[None, :]
    angles = 2.0 * math.pi * phase.astype(F32) / length[None, :].astype(F32)
    return (jnp.cos(angles), jnp.sin(angles))


def tables(local_index, length):
    outer = MW // 2 // RADIX
    a_cos, a_sin = trig(2 * RADIX * lax.iota(jnp.int32, outer), local_index, length)
    b_cos, b_sin = trig(lax.iota(jnp.int32, 2 * RADIX), local_index, length)
    pts = local_index.shape[0]
    b_cos = b_cos.reshape(RADIX, 2, pts).transpose(1, 0, 2)[:, None]
    b_sin = b_sin.reshape(RADIX, 2, pts).transpose(1, 0, 2)[:, None]
    a_cos, a_sin = (a_cos[None, :, None], a_sin[None, :, None])
    cos = (a_cos * b_cos - a_sin * b_sin).astype(BF16).reshape(2, MW // 2, pts)
    sin = (a_sin * b_cos + a_cos * b_sin).astype(BF16).reshape(2, MW // 2, pts)
    return (cos, sin)


def grid_products(grid_values):
    layer_count = grid_values.shape[0] // 4
    u, w, t, q = grid_values.astype(F32).reshape(4, layer_count, grid_values.shape[1])
    level = lax.iota(jnp.int32, layer_count)
    acc, rows = (t[layer_count - 1], [])
    rows.append(acc)
    for v in range(layer_count - 2, -1, -1):
        acc = acc + t[v]
        rows.append(acc)
    geo = jnp.stack(rows[::-1]) / math.sqrt(layer_count)
    energy = 0.5 * (u * u + w * w) + geo
    return jnp.stack([energy, u * t, w * t, u * q]).reshape(grid_values.shape).astype(BF16)


def local(spectral, legendre, pair_ids):
    slots, _, cols, row_total = spectral.shape
    lat_count = legendre.shape[1]
    tiles = lax.axis_size("tile")
    zero = jnp.zeros((), BF16)
    wave_here = lax.axis_index("wave")
    slot_ids = lax.dynamic_slice_in_dim(pair_ids, wave_here * slots, slots)
    row_index = lax.broadcasted_iota(jnp.int32, (slots, row_total), 1)
    upper = (row_index >= (MW - slot_ids)[:, None])[:, None, :]
    masked = jnp.concatenate(
        [jnp.where(upper, zero, legendre), jnp.where(upper, legendre, zero)], axis=1
    )
    spec = spectral.reshape(slots, 2 * cols, row_total)
    cycle_index, cycle_len = cycle_lengths(wave_here, lat_count // 2)
    scales = cycle_scale(cycle_index, cycle_len, lat_count)
    quarter = NPTS // 4
    step = (
        tiles * LANES // math.gcd(4, tiles) if tiles * LANES // math.gcd(4, tiles) <= 512 else 512
    )
    kpad = -(-quarter // step) * step
    k = lax.iota(jnp.int32, kpad)
    q0 = cycle_len[0] // 4
    second = k >= q0
    inside = k < quarter
    local_index = jnp.where(inside, k - jnp.where(second, q0, 0), 0)
    length = jnp.where(second, cycle_len[1], cycle_len[0])
    cos, sin = tables(local_index, length)
    half = MW // 2
    m_order = jnp.arange(MW, dtype=jnp.int32).reshape(half, 2).T
    quarter_m = half // 2
    m0, m1 = (m_order[:, :quarter_m], m_order[:, quarter_m:])
    q_of = jnp.stack([m0, MW - 1 - m1]).reshape(2, half)
    hot = (pair_ids[None, :, None] == q_of[:, None, :]).astype(BF16)
    coefficients = (
        lax.dot_general(masked, spec, (((2,), (2,)), ((0,), (0,))), preferred_element_type=F32)
        .astype(BF16)
        .reshape(slots, 2, lat_count, 2 * cols)
    )
    coefficients = coefficients.transpose(2, 1, 3, 0)
    fourier = lax.all_to_all(coefficients, "wave", split_axis=0, concat_axis=3, tiled=True)
    ordered = lax.dot_general(
        fourier, hot, (((3,), (1,)), ((1,), (0,))), preferred_element_type=F32
    )
    ordered = ordered.reshape(2, 2, 2, cols, 2, quarter_m).transpose(4, 2, 1, 3, 0, 5)
    ordered = ordered.reshape(2, 2, 2, cols, half)
    factor = jnp.where(m_order == 0, 1.0, 2.0).astype(F32)
    keep = 2 * m_order[:, None, :] < cycle_len[None, :, None]
    ordered = ordered * jnp.where(keep, factor[:, None, :], 0.0)[:, None, :, None, :]
    sign = jnp.where(m_order // 2 % 2 == 0, 1.0, -1.0).astype(F32)
    re, im = (ordered[:, 0].reshape(2, 2 * cols, half), ordered[:, 1].reshape(2, 2 * cols, half))
    even_c = jnp.concatenate([re[0], re[0] * sign[0]]).astype(BF16)
    even_s = jnp.concatenate([-im[0], -im[0] * sign[0]]).astype(BF16)
    odd_c = jnp.concatenate([re[1], im[1] * sign[1]]).astype(BF16)
    odd_s = jnp.concatenate([-im[1], re[1] * sign[1]]).astype(BF16)
    dot = functools.partial(jnp.dot, preferred_element_type=F32)
    even = (dot(even_c, cos[0]) + dot(even_s, sin[0])).reshape(2, 2, cols, kpad)
    odd = (dot(odd_c, cos[1]) + dot(odd_s, sin[1])).reshape(2, 2, cols, kpad)
    even = jnp.where(second, even[:, 1], even[:, 0])
    odd = jnp.where(second, odd[:, 1], odd[:, 0])
    grid_values = jnp.stack(
        [even[0] + odd[0], even[1] - odd[1], even[0] - odd[0], even[1] + odd[1]], axis=1
    ).astype(BF16)
    grid_values = grid_values.reshape(cols, 4 * kpad)
    grid_values = lax.all_to_all(grid_values, "tile", split_axis=1, concat_axis=0, tiled=True)
    product = grid_products(grid_values)
    product = lax.all_to_all(product, "tile", split_axis=0, concat_axis=1, tiled=True)
    x = product.astype(F32).reshape(cols, 4, kpad)
    x = jnp.where(inside, x, 0.0)
    x0, x1, x2, x3 = (x[:, 0], x[:, 1], x[:, 2], x[:, 3])

    def by_lat(a, b):
        both = jnp.stack([a, b])[:, None]
        return (
            jnp.where(second == (lax.iota(jnp.int32, 2) == 1)[None, :, None, None], both, 0.0)
            .astype(BF16)
            .reshape(4 * cols, kpad)
        )

    even_in = by_lat(x0 + x2 + (x1 + x3), x0 + x2 - (x1 + x3))
    odd_in = by_lat(x0 - x2, x1 - x3)
    nt = lambda a, b: lax.dot_general(
        a, b, (((1,), (1,)), ((), ())), preferred_element_type=F32
    ).reshape(2, 2, cols, half)
    ec, es = (nt(even_in, cos[0]), nt(even_in, sin[0]))
    oc, os_ = (nt(odd_in, cos[1]), nt(odd_in, sin[1]))
    pick = sign[0] > 0
    even_re = jnp.where(pick, ec[0], ec[1])
    even_im = -jnp.where(pick, es[0], es[1])
    odd_re = oc[0] - sign[1] * os_[1]
    odd_im = -os_[0] - sign[1] * oc[1]
    back = jnp.stack([jnp.stack([even_re, even_im]), jnp.stack([odd_re, odd_im])])
    back = back * jnp.where(keep, scales[None, :, None], 0.0)[:, None, :, None, :]
    back = back.astype(BF16).reshape(2, 2, 2, cols, 2, quarter_m).transpose(4, 2, 1, 3, 0, 5)
    back = back.reshape(2, 4 * cols, half)
    back = lax.dot_general(
        back, hot, (((2,), (2,)), ((0,), (0,))), preferred_element_type=F32
    ).astype(BF16)
    back = back.reshape(2, 2, 2 * cols, PAIRS).transpose(1, 0, 2, 3)
    returned = lax.all_to_all(back, "wave", split_axis=3, concat_axis=0, tiled=True)
    returned = returned.transpose(3, 2, 1, 0).reshape(slots, 2 * cols, 2 * lat_count)
    result = lax.dot_general(
        returned, masked, (((2,), (1,)), ((0,), (0,))), preferred_element_type=F32
    )
    return result.reshape(slots, 2, cols, row_total).astype(BF16)


def solution(mesh):
    placed = (P("wave", None, "tile", None), P("wave", None, None), P())
    return jax.shard_map(
        local, mesh=mesh, in_specs=placed, out_specs=P("wave", None, "tile", None), check_vma=False
    )
```

profile of v0, /device:TPU:0, one launch (start us, length us, event | category | flops | bytes accessed | tf_op | source)
XLA Modules:
  0.0 97.7 jit_solution(9886017591165895922)
XLA Ops:
  0.0 0.8 dynamic-slice_subtract_fusion
  1.0 5.1 %broadcast_select_fusion.1 = (bf16[160,8,1281]{2,1,0:T(8,128)(2,1)}, bf16[160,8,1281]{2,1,0:T(8,128)(2,1)}) fusion(bf16[160,8,1281]{2,1,0:T(8,128)(2,1)} %param.4, pred[160,1281]{1,0:T(8,128)(4,1)S(1)} %iota_compare_fusion), kind=kLoop, calls=%fused_computation.10 | loop fusion | flops 3279360 | bytes 10043040 | tf_op jit(solution)/shard_map/jit(_where)/select_n | solution.py:72
  6.1 8.6 %fusion.12 = bf16[160,2,8,16]{3,2,1,0:T(8,128)(2,1)S(1)} fusion(bf16[160,2,8,1281]{3,2,1,0:T(8,128)(2,1)} %param.3, bf16[160,8,1281]{2,1,0:T(8,128)(2,1)} %get-tuple-element.27, bf16[160,8,1281]{2,1,0:T(8,128)(2,1)} %get-tuple-element.26), kind=kOutput, calls=%fused_computation.19 | convolution fusion | flops 118097920 | bytes 13199360 | tf_op jit(solution)/shard_map/dot_general | solution.py:96
  14.6 1.2 %copy.44 = bf16[160,2,8,16]{0,3,1,2:T(8,128)(2,1)} copy(bf16[160,2,8,16]{3,2,1,0:T(8,128)(2,1)S(1)} %fusion.12) | data formatting | bytes 163840 | tf_op jit(solution)/shard_map/reshape | solution.py:98
  15.9 6.3 %all-to-all-start = ((bf16[8,2,16,160]{3,2,1,0:T(8,128)(2,1)}), bf16[8,2,16,160]{3,2,1,0:T(8,128)(2,1)S(1)}, u32[]{:S(2)}, u32[]{:S(2)}) async-start(bf16[8,2,16,160]{3,2,1,0:T(8,128)(2,1)} %bitcast.5), calls=%async_computation | async-start | bytes 262144 | tf_op jit(solution)/shard_map/all_to_all | solution.py:101
  22.4 0.6 fusion.82
  25.6 1.3 %iota_compare_fusion.2 = (pred[1536]{0:T(1024)(128)(4,1)S(1)}, pred[1536]{0:T(1024)(128)(4,1)S(1)}) fusion(s32[]{:T(128)S(6)} %select_n.232, s32[]{:T(128)} %bitcast.2, s32[]{:T(128)} %bitcast.13), kind=kLoop, calls=%fused_computation.136 | loop fusion | flops 7680 | bytes 3084 | tf_op jit(solution)/shard_map/ge | solution.py:84
  26.9 1.3 %compare_select_fusion.1 = (s32[1536]{0:T(1024)S(1)}, f32[1536]{0:T(1024)S(1)}) fusion(s32[]{:T(128)} %bitcast.2, s32[]{:T(128)} %bitcast.13, s32[]{:T(128)S(6)} %select_n.232), kind=kLoop, calls=%fused_computation.123 | loop fusion | flops 7680 | bytes 12300 | tf_op jit(solution)/shard_map/jit(remainder)/jit(_where)/select_n | solution.py:30
  28.3 2.1 %fusion.39 = (f32[20,1536]{1,0:T(8,128)S(1)}, f32[20,1536]{1,0:T(8,128)S(1)}) fusion(f32[1536]{0:T(1024)S(1)} %get-tuple-element.78, pred[1536]{0:T(1024)(128)(4,1)S(1)} %get-tuple-element.80, s32[1536]{0:T(1024)S(1)} %get-tuple-element.77, s32[1536]{0:T(1024)S(1)} %subtract_select_fusion, s32[20]{0:T(128)S(1)} %iota_multiply_fusion), kind=kLoop, calls=%fused_computation.65 | loop fusion | flops 337920 | bytes 265808 | tf_op jit(solution)/shard_map/cos | solution.py:32
  30.3 5.3 %fusion.27 = (f32[2,32,1536]{2,1,0:T(8,128)S(1)}, f32[2,32,1536]{2,1,0:T(8,128)S(1)}) fusion(f32[1536]{0:T(1024)S(1)} %get-tuple-element.78, pred[1536]{0:T(1024)(128)(4,1)S(1)} %get-tuple-element.80, s32[1536]{0:T(1024)S(1)} %get-tuple-element.77, s32[1536]{0:T(1024)S(1)} %subtract_select_fusion, s32[2,32]{1,0:T(2,128)S(1)} %multiply_add_fusion.1), kind=kLoop, calls=%fused_computation.40 | loop fusion | flops 1081344 | bytes 806656 | tf_op jit(solution)/shard_map/cos | solution.py:32
  35.6 2.5 %add_convert_fusion = (bf16[2,20,32,1536]{3,2,1,0:T(8,128)(2,1)S(1)}, bf16[2,20,32,1536]{3,2,1,0:T(8,128)(2,1)S(1)}) fusion(f32[2,32,1536]{2,1,0:T(8,128)S(1)} %get-tuple-element.62, f32[20,1536]{1,0:T(8,128)S(1)} %get-tuple-element.64, f32[2,32,1536]{2,1,0:T(8,128)S(1)} %get-tuple-element.61, f32[20,1536]{1,0:T(8,128)S(1)} %get-tuple-element.63), kind=kLoop, calls=%fused_computation | loop fusion | flops 15728640 | bytes 8896512 | tf_op jit(solution)/shard_map/convert_element_type | solution.py:44
  38.1 1.5 %fusion.75 = (bf16[1,20,32,1536]{3,2,1,0:T(8,128)(2,1)}, bf16[1,20,32,1536]{3,2,1,0:T(8,128)(2,1)S(1)}) fusion(bf16[2,20,32,1536]{3,2,1,0:T(8,128)(2,1)S(1)} %get-tuple-element.28), kind=kLoop, calls=%fused_computation.178 | loop fusion | bytes 7864320 | tf_op jit(solution)/shard_map/slice | solution.py:117
  39.6 2.3 %fusion.76 = (bf16[1,20,32,1536]{3,2,1,0:T(8,128)(2,1)}, bf16[1,20,32,1536]{3,2,1,0:T(8,128)(2,1)}) fusion(bf16[2,20,32,1536]{3,2,1,0:T(8,128)(2,1)S(1)} %get-tuple-element.29), kind=kLoop, calls=%fused_computation.179 | loop fusion | bytes 7864320 | tf_op jit(solution)/shard_map/slice | solution.py:117
  42.7 0.7 fusion.4
  44.0 2.1 %fusion.43 = f32[32,1536]{1,0:T(8,128)S(1)} fusion(bf16[640,1536]{1,0:T(8,128)(2,1)} %bitcast.174, bf16[16,640]{1,0:T(8,128)(2,1)S(1)} %get-tuple-element.43, bf16[16,640]{1,0:T(8,128)(2,1)S(1)} %get-tuple-element.49), kind=kOutput, calls=%fused_computation.92 | convolution fusion | flops 62996480 | bytes 2203648 | tf_op jit(solution)/shard_map/dot_general | solution.py:117
  46.1 2.0 %fusion.50 = f32[32,1536]{1,0:T(8,128)S(1)} fusion(bf16[640,1536]{1,0:T(8,128)(2,1)} %bitcast.170, bf16[16,640]{1,0:T(8,128)(2,1)S(1)} %get-tuple-element.47, bf16[16,640]{1,0:T(8,128)(2,1)S(1)} %get-tuple-element.50), kind=kOutput, calls=%fused_computation.99 | convolution fusion | flops 62996480 | bytes 2203648 | tf_op jit(solution)/shard_map/dot_general | solution.py:118
  49.1 0.7 pad_maximum_fusion.7
  49.8 3.7 %all-to-all-start.1 = ((bf16[8,8,768]{2,0,1:T(8,128)(2,1)}), bf16[8,8,768]{2,0,1:T(8,128)(2,1)S(1)}, u32[]{:S(2)}, u32[]{:S(2)}) async-start(bf16[8,8,768]{2,0,1:T(8,128)(2,1)} %bitcast.31), calls=%async_computation.1 | async-start | bytes 196608 | tf_op jit(solution)/shard_map/all_to_all | solution.py:125
  53.6 5.1 %all-to-all-done.1 = bf16[8,8,768]{2,0,1:T(8,128)(2,1)S(1)} async-done(((bf16[8,8,768]{2,0,1:T(8,128)(2,1)}), bf16[8,8,768]{2,0,1:T(8,128)(2,1)S(1)}, u32[]{:S(2)}, u32[]{:S(2)}) %all-to-all-start.1) | async-done | bytes 98336 | tf_op jit(solution)/shard_map/all_to_all | solution.py:125
  58.9 0.7 pad_maximum_fusion.8
  59.6 3.4 %all-to-all-start.2 = ((bf16[8,8,768]{2,1,0:T(8,128)(2,1)}), bf16[8,8,768]{2,1,0:T(8,128)(2,1)S(1)}, u32[]{:S(2)}, u32[]{:S(2)}) async-start(bf16[8,8,768]{2,1,0:T(8,128)(2,1)} %bitcast.40), calls=%async_computation.2 | async-start | bytes 196608 | tf_op jit(solution)/shard_map/all_to_all | solution.py:127
  62.9 5.1 %all-to-all-done.2 = bf16[8,8,768]{2,1,0:T(8,128)(2,1)S(1)} async-done(((bf16[8,8,768]{2,1,0:T(8,128)(2,1)}), bf16[8,8,768]{2,1,0:T(8,128)(2,1)S(1)}, u32[]{:S(2)}, u32[]{:S(2)}) %all-to-all-start.2) | async-done | bytes 98336 | tf_op jit(solution)/shard_map/all_to_all | solution.py:127
  68.2 2.3 %fusion.84 = f32[32,640]{1,0:T(8,128)S(1)} fusion(bf16[32,1536]{1,0:T(8,128)(2,1)S(1)} %bitcast.179, bf16[640,1536]{1,0:T(8,128)(2,1)} %bitcast.172), kind=kOutput, calls=%fused_computation.188 | convolution fusion | flops 62914560 | bytes 2146304 | tf_op jit(solution)/shard_map/dot_general | solution.py:142
  70.6 0.7 fusion.83
  71.2 0.7 fusion.86
  71.9 0.7 fusion.85
  73.9 0.7 fusion.15
  74.7 0.9 copy.54
  76.0 0.7 reshape.950
  76.7 10.7 %all_to_all.56 = bf16[4,2,5120]{2,1,0:T(2,128)(2,1)S(1)} all-to-all(bf16[4,2,5120]{2,1,0:T(2,128)(2,1)S(1)} %reshape.950), channel_id=1, replica_groups=mesh['wave'=4,'tile'=8] {'wave'}, dimensions={0} | all-to-all | bytes 163840 | tf_op jit(solution)/shard_map/all_to_all | solution.py:160
  87.8 0.9 copy.60
  89.4 8.3 %convert_bitcast_fusion = bf16[160,2,8,1281]{3,2,1,0:T(8,128)(2,1)} fusion(bf16[160,16,16]{2,1,0:T(8,128)(2,1)S(1)} %copy.58, bf16[160,8,1281]{2,1,0:T(8,128)(2,1)} %get-tuple-element.27, bf16[160,8,1281]{2,1,0:T(8,128)(2,1)} %get-tuple-element.26), kind=kOutput, calls=%fused_computation.5 | convolution fusion | flops 121336320 | bytes 13199360 | tf_op jit(solution)/shard_map/dot_general | solution.py:162
  (81 shorter events, 6.1 us)
Async XLA Ops:
  15.9 26.6 %all-to-all-start = ((bf16[8,2,16,160]{3,2,1,0:T(8,128)(2,1)}), bf16[8,2,16,160]{3,2,1,0:T(8,128)(2,1)S(1)}, u32[]{:S(2)}, u32[]{:S(2)}) async-start(bf16[8,2,16,160]{3,2,1,0:T(8,128)(2,1)} %bitcast.5), calls=%async_computation | async-start | bytes 262144 | tf_op jit(solution)/shard_map/all_to_all | solution.py:101
  39.6 3.0 %copy-start.3 = (s32[640]{0:T(1024)S(1)}, s32[640]{0:T(1024)}, u32[]{:S(2)}) copy-start(s32[640]{0:T(1024)} %param.5) | copy-start | bytes 7684
  43.9 4.2 %copy-start.1 = (bf16[1,20,32,1536]{3,2,1,0:T(8,128)(2,1)S(1)}, bf16[1,20,32,1536]{3,2,1,0:T(8,128)(2,1)}, u32[]{:S(2)}) copy-start(bf16[1,20,32,1536]{3,2,1,0:T(8,128)(2,1)} %get-tuple-element.22) | copy-start | bytes 5898244
  49.8 8.9 %all-to-all-start.1 = ((bf16[8,8,768]{2,0,1:T(8,128)(2,1)}), bf16[8,8,768]{2,0,1:T(8,128)(2,1)S(1)}, u32[]{:S(2)}, u32[]{:S(2)}) async-start(bf16[8,8,768]{2,0,1:T(8,128)(2,1)} %bitcast.31), calls=%async_computation.1 | async-start | bytes 196608 | tf_op jit(solution)/shard_map/all_to_all | solution.py:125
  59.6 8.5 %all-to-all-start.2 = ((bf16[8,8,768]{2,1,0:T(8,128)(2,1)}), bf16[8,8,768]{2,1,0:T(8,128)(2,1)S(1)}, u32[]{:S(2)}, u32[]{:S(2)}) async-start(bf16[8,8,768]{2,1,0:T(8,128)(2,1)} %bitcast.40), calls=%async_computation.2 | async-start | bytes 196608 | tf_op jit(solution)/shard_map/all_to_all | solution.py:127
  68.0 2.5 %copy-start.2 = (bf16[1,20,32,1536]{3,2,1,0:T(8,128)(2,1)S(1)}, bf16[1,20,32,1536]{3,2,1,0:T(8,128)(2,1)}, u32[]{:S(2)}) copy-start(bf16[1,20,32,1536]{3,2,1,0:T(8,128)(2,1)} %get-tuple-element.24) | copy-start | bytes 5898244
  68.1 3.8 %copy-start = (bf16[1,20,32,1536]{3,2,1,0:T(8,128)(2,1)S(1)}, bf16[1,20,32,1536]{3,2,1,0:T(8,128)(2,1)}, u32[]{:S(2)}) copy-start(bf16[1,20,32,1536]{3,2,1,0:T(8,128)(2,1)} %get-tuple-element.25) | copy-start | bytes 5898244
where the time goes:
time: 98.3 us; the launch traced here: 97.7 us
  matrix products  27.7 us (28%)
  other arithmetic  20.9 us (21%)
  starting transfers between devices  13.4 us (14%)
  local copies, waits for them, and re-layouts  11.9 us (12%)
  blocking collectives  10.7 us (11%)
  waiting for transfers between devices  10.2 us (10%)
  between operations  3 us (3%)
    all_to_all x1, blocking collectives, local(): lax.all_to_all(back, 'wave', split_axis=3, concat_axis=0, tiled=True)  10.7 us
    dot_general x1, matrix products, local(): lax.dot_general(masked, spec, (((2,), (2,)), ((0,), (0,))), preferred_ele...  8.57 us
    dot_general x1, matrix products, local(): lax.dot_general(returned, masked, (((2,), (1,)), ((0,), (0,))), preferred...  8.31 us
    cos x2, other arithmetic, trig(): return (jnp.cos(angles), jnp.sin(angles))  7.33 us
    all_to_all x1, starting transfers between devices, local(): lax.all_to_all(coefficients, 'wave', split_axis=0, concat_axis=3, tiled=T...  6.35 us
    all_to_all x1, waiting for transfers between devices, local(): lax.all_to_all(product, 'tile', split_axis=0, concat_axis=1, tiled=True)  5.11 us
    select_n x1, other arithmetic, local(): jnp.where(upper, zero, legendre)  5.11 us
    all_to_all x1, waiting for transfers between devices, local(): lax.all_to_all(grid_values, 'tile', split_axis=1, concat_axis=0, tiled=True)  5.08 us
  transfers between devices with their start and end apart: 3, of which 2 were waited for; matrix products, arithmetic and copies ran while one was open for 18% of the time, Pallas kernels for 0%

commit v1 on v0

--- a/solution.py
+++ b/solution.py
@@ -13,6 +13,17 @@
 RADIX = 32
 F32 = jnp.float32
 BF16 = jnp.bfloat16
+
+
+def split_up(value, dim, size):
+    before, after = (value.shape[:dim], value.shape[dim + 1 :])
+    return jnp.moveaxis(value.reshape(*before, size, -1, *after), dim, 0)
+
+
+def in_order(tiles, dim):
+    tiles = jnp.moveaxis(tiles, 0, dim)
+    dims = tiles.shape
+    return tiles.reshape(*dims[:dim], dims[dim] * dims[dim + 1], *dims[dim + 2 :])
 
 
 def cycle_lengths(pair_number, pair_total):
@@ -157,7 +168,16 @@
         back, hot, (((2,), (2,)), ((0,), (0,))), preferred_element_type=F32
     ).astype(BF16)
     back = back.reshape(2, 2, 2 * cols, PAIRS).transpose(1, 0, 2, 3)
-    returned = lax.all_to_all(back, "wave", split_axis=3, concat_axis=0, tiled=True)
+    length_2, mine = (lax.axis_size("wave"), lax.axis_index("wave"))
+    pieces = split_up(back, 3, length_2)
+    done = [pieces[mine]]
+    for step_2 in range(1, length_2):
+        sent = pieces[(mine + step_2) % length_2]
+        done.append(
+            lax.ppermute(sent, "wave", [(i, (i + step_2) % length_2) for i in range(length_2)])
+        )
+    pieces = jnp.stack(done)[(mine - jnp.arange(length_2)) % length_2]
+    returned = in_order(pieces, 0)
     returned = returned.transpose(3, 2, 1, 0).reshape(slots, 2 * cols, 2 * lat_count)
     result = lax.dot_general(
         returned, masked, (((2,), (1,)), ((0,), (0,))), preferred_element_type=F32

time: 98.3 us -> 94.4 us (0.960)
  blocking collectives: 10.7 us -> 0 us
  starting transfers between devices: 13.4 us -> 19.3 us
  waiting for transfers between devices: 10.2 us -> 12.7 us
  local copies, waits for them, and re-layouts: 11.9 us -> 9.55 us
    all_to_all x1 -> x0, blocking collectives: 10.7 us -> none  [local(): lax.all_to_all(back, 'wave', split_axis=3, concat_axis=0, tiled=True)]
    ppermute x0 -> x3, starting transfers between devices: none -> 5.91 us  [local(): lax.ppermute(sent, 'wave', [(i, (i + step_2) % length_2) for i in range(l...]
    ppermute x0 -> x3, waiting for transfers between devices: none -> 2.42 us  [local(): lax.ppermute(sent, 'wave', [(i, (i + step_2) % length_2) for i in range(l...]
    unnamed x12 -> x13, local copies, waits for them, and re-layouts: 1.62 us -> 0.05 us
  transfers between devices with their start and end apart: 3 -> 6, of which waited for: 2 -> 4; matrix products, arithmetic and copies ran while one was open for 18% -> 19% of each run, Pallas kernels for 0% -> 0%
where the time goes in v1:
time: 94.4 us; the launch traced here: 93.9 us
  matrix products  27.7 us (29%)
  other arithmetic  21.3 us (23%)
  starting transfers between devices  19.3 us (20%)
  waiting for transfers between devices  12.7 us (13%)
  local copies, waits for them, and re-layouts  9.55 us (10%)
  between operations  3.35 us (4%)
    dot_general x1, matrix products, local(): lax.dot_general(masked, spec, (((2,), (2,)), ((0,), (0,))), preferred_ele...  8.57 us
    dot_general x1, matrix products, local(): lax.dot_general(returned, masked, (((2,), (1,)), ((0,), (0,))), preferred...  8.31 us
    cos x2, other arithmetic, trig(): return (jnp.cos(angles), jnp.sin(angles))  7.33 us
    all_to_all x1, starting transfers between devices, local(): lax.all_to_all(coefficients, 'wave', split_axis=0, concat_axis=3, tiled=T...  6.35 us
    ppermute x3, starting transfers between devices, local(): lax.ppermute(sent, 'wave', [(i, (i + step_2) % length_2) for i in range(l...  5.91 us
    all_to_all x1, waiting for transfers between devices, local(): lax.all_to_all(grid_values, 'tile', split_axis=1, concat_axis=0, tiled=True)  5.19 us
    select_n x1, other arithmetic, local(): jnp.where(upper, zero, legendre)  5.11 us
    all_to_all x1, waiting for transfers between devices, local(): lax.all_to_all(product, 'tile', split_axis=0, concat_axis=1, tiled=True)  5.11 us
  transfers between devices with their start and end apart: 6, of which 4 were waited for; matrix products, arithmetic and copies ran while one was open for 19% of the time, Pallas kernels for 0%

profile of v1, /device:TPU:0, one launch (start us, length us, event | category | flops | bytes accessed | tf_op | source)
XLA Modules:
  0.0 93.9 jit_solution(15574525387759677815)
XLA Ops:
  0.0 0.8 dynamic-slice_subtract_fusion
  1.0 5.1 %broadcast_select_fusion.1 = (bf16[160,8,1281]{2,1,0:T(8,128)(2,1)}, bf16[160,8,1281]{2,1,0:T(8,128)(2,1)}) fusion(bf16[160,8,1281]{2,1,0:T(8,128)(2,1)} %param.4, pred[160,1281]{1,0:T(8,128)(4,1)S(1)} %iota_compare_fusion), kind=kLoop, calls=%fused_computation.11 | loop fusion | flops 3279360 | bytes 10043040 | tf_op jit(solution)/shard_map/jit(_where)/select_n | solution.py:83
  6.1 8.6 %fusion.12 = bf16[160,2,8,16]{3,2,1,0:T(8,128)(2,1)S(1)} fusion(bf16[160,2,8,1281]{3,2,1,0:T(8,128)(2,1)} %param.3, bf16[160,8,1281]{2,1,0:T(8,128)(2,1)} %get-tuple-element.27, bf16[160,8,1281]{2,1,0:T(8,128)(2,1)} %get-tuple-element.26), kind=kOutput, calls=%fused_computation.20 | convolution fusion | flops 118097920 | bytes 13199360 | tf_op jit(solution)/shard_map/dot_general | solution.py:107
  14.6 1.2 %copy.42 = bf16[160,2,8,16]{0,3,1,2:T(8,128)(2,1)} copy(bf16[160,2,8,16]{3,2,1,0:T(8,128)(2,1)S(1)} %fusion.12) | data formatting | bytes 163840 | tf_op jit(solution)/shard_map/reshape | solution.py:109
  15.9 6.3 %all-to-all-start = ((bf16[8,2,16,160]{3,2,1,0:T(8,128)(2,1)}), bf16[8,2,16,160]{3,2,1,0:T(8,128)(2,1)S(1)}, u32[]{:S(2)}, u32[]{:S(2)}) async-start(bf16[8,2,16,160]{3,2,1,0:T(8,128)(2,1)} %bitcast.5), calls=%async_computation | async-start | bytes 262144 | tf_op jit(solution)/shard_map/all_to_all | solution.py:112
  25.9 1.3 %iota_compare_fusion.2 = (pred[1536]{0:T(1024)(128)(4,1)S(1)}, pred[1536]{0:T(1024)(128)(4,1)S(1)}) fusion(s32[]{:T(128)S(6)} %select_n.281, s32[]{:T(128)} %bitcast.2, s32[]{:T(128)} %bitcast.13), kind=kLoop, calls=%fused_computation.143 | loop fusion | flops 7680 | bytes 3084 | tf_op jit(solution)/shard_map/ge | solution.py:95
  27.3 1.3 %compare_select_fusion.1 = (s32[1536]{0:T(1024)S(1)}, f32[1536]{0:T(1024)S(1)}) fusion(s32[]{:T(128)} %bitcast.2, s32[]{:T(128)} %bitcast.13, s32[]{:T(128)S(6)} %select_n.281), kind=kLoop, calls=%fused_computation.130 | loop fusion | flops 7680 | bytes 12300 | tf_op jit(solution)/shard_map/jit(remainder)/jit(_where)/select_n | solution.py:41
  28.7 2.1 %fusion.39 = (f32[20,1536]{1,0:T(8,128)S(1)}, f32[20,1536]{1,0:T(8,128)S(1)}) fusion(f32[1536]{0:T(1024)S(1)} %get-tuple-element.82, pred[1536]{0:T(1024)(128)(4,1)S(1)} %get-tuple-element.84, s32[1536]{0:T(1024)S(1)} %get-tuple-element.81, s32[1536]{0:T(1024)S(1)} %subtract_select_fusion, s32[20]{0:T(128)S(1)} %iota_multiply_fusion), kind=kLoop, calls=%fused_computation.68 | loop fusion | flops 337920 | bytes 265808 | tf_op jit(solution)/shard_map/cos | solution.py:43
  30.8 5.3 %fusion.27 = (f32[2,32,1536]{2,1,0:T(8,128)S(1)}, f32[2,32,1536]{2,1,0:T(8,128)S(1)}) fusion(f32[1536]{0:T(1024)S(1)} %get-tuple-element.82, pred[1536]{0:T(1024)(128)(4,1)S(1)} %get-tuple-element.84, s32[1536]{0:T(1024)S(1)} %get-tuple-element.81, s32[1536]{0:T(1024)S(1)} %subtract_select_fusion, s32[2,32]{1,0:T(2,128)S(1)} %multiply_add_fusion.1), kind=kLoop, calls=%fused_computation.41 | loop fusion | flops 1081344 | bytes 806656 | tf_op jit(solution)/shard_map/cos | solution.py:43
  36.1 2.7 %add_convert_fusion = (bf16[2,20,32,1536]{3,2,1,0:T(8,128)(2,1)S(1)}, bf16[2,20,32,1536]{3,2,1,0:T(8,128)(2,1)S(1)}) fusion(f32[2,32,1536]{2,1,0:T(8,128)S(1)} %get-tuple-element.66, f32[20,1536]{1,0:T(8,128)S(1)} %get-tuple-element.68, f32[2,32,1536]{2,1,0:T(8,128)S(1)} %get-tuple-element.65, f32[20,1536]{1,0:T(8,128)S(1)} %get-tuple-element.67), kind=kLoop, calls=%fused_computation.1 | loop fusion | flops 15728640 | bytes 8896512 | tf_op jit(solution)/shard_map/convert_element_type | solution.py:55
  38.8 1.5 %fusion.77 = (bf16[1,20,32,1536]{3,2,1,0:T(8,128)(2,1)}, bf16[1,20,32,1536]{3,2,1,0:T(8,128)(2,1)S(1)}) fusion(bf16[2,20,32,1536]{3,2,1,0:T(8,128)(2,1)S(1)} %get-tuple-element.28), kind=kLoop, calls=%fused_computation.196 | loop fusion | bytes 7864320 | tf_op jit(solution)/shard_map/slice | solution.py:128
  40.3 2.3 %fusion.78 = (bf16[1,20,32,1536]{3,2,1,0:T(8,128)(2,1)}, bf16[1,20,32,1536]{3,2,1,0:T(8,128)(2,1)}) fusion(bf16[2,20,32,1536]{3,2,1,0:T(8,128)(2,1)S(1)} %get-tuple-element.29), kind=kLoop, calls=%fused_computation.197 | loop fusion | bytes 7864320 | tf_op jit(solution)/shard_map/slice | solution.py:128
  43.5 0.7 fusion.4
  44.8 2.1 %fusion.43 = f32[32,1536]{1,0:T(8,128)S(1)} fusion(bf16[640,1536]{1,0:T(8,128)(2,1)} %bitcast.189, bf16[16,640]{1,0:T(8,128)(2,1)S(1)} %get-tuple-element.43, bf16[16,640]{1,0:T(8,128)(2,1)S(1)} %get-tuple-element.49), kind=kOutput, calls=%fused_computation.95 | convolution fusion | flops 62996480 | bytes 2203648 | tf_op jit(solution)/shard_map/dot_general | solution.py:128
  46.9 2.0 %fusion.50 = f32[32,1536]{1,0:T(8,128)S(1)} fusion(bf16[640,1536]{1,0:T(8,128)(2,1)} %bitcast.185, bf16[16,640]{1,0:T(8,128)(2,1)S(1)} %get-tuple-element.47, bf16[16,640]{1,0:T(8,128)(2,1)S(1)} %get-tuple-element.50), kind=kOutput, calls=%fused_computation.102 | convolution fusion | flops 62996480 | bytes 2203648 | tf_op jit(solution)/shard_map/dot_general | solution.py:129
  49.9 0.6 pad_maximum_fusion.8
  50.6 3.7 %all-to-all-start.1 = ((bf16[8,8,768]{2,0,1:T(8,128)(2,1)}), bf16[8,8,768]{2,0,1:T(8,128)(2,1)S(1)}, u32[]{:S(2)}, u32[]{:S(2)}) async-start(bf16[8,8,768]{2,0,1:T(8,128)(2,1)} %bitcast.31), calls=%async_computation.1 | async-start | bytes 196608 | tf_op jit(solution)/shard_map/all_to_all | solution.py:136
  54.3 5.2 %all-to-all-done.1 = bf16[8,8,768]{2,0,1:T(8,128)(2,1)S(1)} async-done(((bf16[8,8,768]{2,0,1:T(8,128)(2,1)}), bf16[8,8,768]{2,0,1:T(8,128)(2,1)S(1)}, u32[]{:S(2)}, u32[]{:S(2)}) %all-to-all-start.1) | async-done | bytes 98336 | tf_op jit(solution)/shard_map/all_to_all | solution.py:136
  59.7 0.6 pad_maximum_fusion.9
  60.4 3.4 %all-to-all-start.2 = ((bf16[8,8,768]{2,1,0:T(8,128)(2,1)}), bf16[8,8,768]{2,1,0:T(8,128)(2,1)S(1)}, u32[]{:S(2)}, u32[]{:S(2)}) async-start(bf16[8,8,768]{2,1,0:T(8,128)(2,1)} %bitcast.40), calls=%async_computation.2 | async-start | bytes 196608 | tf_op jit(solution)/shard_map/all_to_all | solution.py:138
  63.7 5.1 %all-to-all-done.2 = bf16[8,8,768]{2,1,0:T(8,128)(2,1)S(1)} async-done(((bf16[8,8,768]{2,1,0:T(8,128)(2,1)}), bf16[8,8,768]{2,1,0:T(8,128)(2,1)S(1)}, u32[]{:S(2)}, u32[]{:S(2)}) %all-to-all-start.2) | async-done | bytes 98336 | tf_op jit(solution)/shard_map/all_to_all | solution.py:138
  69.0 2.3 %fusion.86 = f32[32,640]{1,0:T(8,128)S(1)} fusion(bf16[32,1536]{1,0:T(8,128)(2,1)S(1)} %bitcast.193, bf16[640,1536]{1,0:T(8,128)(2,1)} %bitcast.187), kind=kOutput, calls=%fused_computation.205 | convolution fusion | flops 62914560 | bytes 2146304 | tf_op jit(solution)/shard_map/dot_general | solution.py:153
  71.4 0.7 fusion.85
  72.0 0.7 fusion.88
  72.7 0.7 fusion.87
  74.7 0.7 fusion.15
  76.0 2.1 %collective-permute-start = (bf16[2,2,16,160]{3,2,1,0:T(8,128)(2,1)S(1)}, bf16[2,2,16,160]{3,2,1,0:T(8,128)(2,1)S(1)}, u32[]{:S(2)}, u32[]{:S(2)}) collective-permute-start(bf16[2,2,16,160]{3,2,1,0:T(8,128)(2,1)S(1)} %bitcast.215), channel_id=1, source_target_pairs={{0,8},{8,16},{16,24},{24,0},{1,9},{9,17},{17,25},{25,1},{2,10},{10... | collective-permute-start | bytes 61448 | tf_op jit(solution)/shard_map/ppermute | solution.py:177
  78.1 2.4 %collective-permute-start.1 = (bf16[2,2,16,160]{3,2,1,0:T(8,128)(2,1)S(1)}, bf16[2,2,16,160]{3,2,1,0:T(8,128)(2,1)S(1)}, u32[]{:S(2)}, u32[]{:S(2)}) collective-permute-start(bf16[2,2,16,160]{3,2,1,0:T(8,128)(2,1)S(1)} %bitcast.214), channel_id=1, source_target_pairs={{0,16},{8,24},{16,0},{24,8},{1,17},{9,25},{17,1},{25,9},{2,18},{10... | collective-permute-start | bytes 61448 | tf_op jit(solution)/shard_map/ppermute | solution.py:177
  80.4 1.5 %collective-permute-start.2 = (bf16[2,2,16,160]{3,2,1,0:T(8,128)(2,1)S(1)}, bf16[2,2,16,160]{3,2,1,0:T(8,128)(2,1)S(1)}, u32[]{:S(2)}, u32[]{:S(2)}) collective-permute-start(bf16[2,2,16,160]{3,2,1,0:T(8,128)(2,1)S(1)} %bitcast.213), channel_id=1, source_target_pairs={{0,24},{8,0},{16,8},{24,16},{1,25},{9,1},{17,9},{25,17},{2,26},{10... | collective-permute-start | bytes 61448 | tf_op jit(solution)/shard_map/ppermute | solution.py:177
  81.9 1.0 %collective-permute-done.1 = bf16[2,2,16,160]{3,2,1,0:T(8,128)(2,1)S(1)} collective-permute-done((bf16[2,2,16,160]{3,2,1,0:T(8,128)(2,1)S(1)}, bf16[2,2,16,160]{3,2,1,0:T(8,128)(2,1)S(1)}, u32[]{:S(2)}, u32[]{:S(2)}) %collective-permute-start.1) | collective-permute-done | bytes 20512 | tf_op jit(solution)/shard_map/ppermute | solution.py:177
  82.9 1.5 %collective-permute-done.2 = bf16[2,2,16,160]{3,2,1,0:T(8,128)(2,1)S(1)} collective-permute-done((bf16[2,2,16,160]{3,2,1,0:T(8,128)(2,1)S(1)}, bf16[2,2,16,160]{3,2,1,0:T(8,128)(2,1)S(1)}, u32[]{:S(2)}, u32[]{:S(2)}) %collective-permute-start.2) | collective-permute-done | bytes 20512 | tf_op jit(solution)/shard_map/ppermute | solution.py:177
  85.6 8.3 %convert_bitcast_fusion = bf16[160,2,8,1281]{3,2,1,0:T(8,128)(2,1)} fusion(bf16[160,16,16]{2,1,0:T(8,128)(2,1)S(1)} %copy.54, bf16[160,8,1281]{2,1,0:T(8,128)(2,1)} %get-tuple-element.27, bf16[160,8,1281]{2,1,0:T(8,128)(2,1)} %get-tuple-element.26), kind=kOutput, calls=%fused_computation.6 | convolution fusion | flops 121336320 | bytes 13199360 | tf_op jit(solution)/shard_map/dot_general | solution.py:182
  (91 shorter events, 6.8 us)
Async XLA Ops:
  15.9 27.4 %all-to-all-start = ((bf16[8,2,16,160]{3,2,1,0:T(8,128)(2,1)}), bf16[8,2,16,160]{3,2,1,0:T(8,128)(2,1)S(1)}, u32[]{:S(2)}, u32[]{:S(2)}) async-start(bf16[8,2,16,160]{3,2,1,0:T(8,128)(2,1)} %bitcast.5), calls=%async_computation | async-start | bytes 262144 | tf_op jit(solution)/shard_map/all_to_all | solution.py:112
  40.3 3.2 %copy-start.3 = (s32[640]{0:T(1024)S(1)}, s32[640]{0:T(1024)}, u32[]{:S(2)}) copy-start(s32[640]{0:T(1024)} %param.5) | copy-start | bytes 7684
  44.7 4.2 %copy-start.1 = (bf16[1,20,32,1536]{3,2,1,0:T(8,128)(2,1)S(1)}, bf16[1,20,32,1536]{3,2,1,0:T(8,128)(2,1)}, u32[]{:S(2)}) copy-start(bf16[1,20,32,1536]{3,2,1,0:T(8,128)(2,1)} %get-tuple-element.22) | copy-start | bytes 5898244
  50.6 8.9 %all-to-all-start.1 = ((bf16[8,8,768]{2,0,1:T(8,128)(2,1)}), bf16[8,8,768]{2,0,1:T(8,128)(2,1)S(1)}, u32[]{:S(2)}, u32[]{:S(2)}) async-start(bf16[8,8,768]{2,0,1:T(8,128)(2,1)} %bitcast.31), calls=%async_computation.1 | async-start | bytes 196608 | tf_op jit(solution)/shard_map/all_to_all | solution.py:136
  60.4 8.5 %all-to-all-start.2 = ((bf16[8,8,768]{2,1,0:T(8,128)(2,1)}), bf16[8,8,768]{2,1,0:T(8,128)(2,1)S(1)}, u32[]{:S(2)}, u32[]{:S(2)}) async-start(bf16[8,8,768]{2,1,0:T(8,128)(2,1)} %bitcast.40), calls=%async_computation.2 | async-start | bytes 196608 | tf_op jit(solution)/shard_map/all_to_all | solution.py:138
  68.9 2.5 %copy-start.2 = (bf16[1,20,32,1536]{3,2,1,0:T(8,128)(2,1)S(1)}, bf16[1,20,32,1536]{3,2,1,0:T(8,128)(2,1)}, u32[]{:S(2)}) copy-start(bf16[1,20,32,1536]{3,2,1,0:T(8,128)(2,1)} %get-tuple-element.24) | copy-start | bytes 5898244
  68.9 3.8 %copy-start = (bf16[1,20,32,1536]{3,2,1,0:T(8,128)(2,1)S(1)}, bf16[1,20,32,1536]{3,2,1,0:T(8,128)(2,1)}, u32[]{:S(2)}) copy-start(bf16[1,20,32,1536]{3,2,1,0:T(8,128)(2,1)} %get-tuple-element.25) | copy-start | bytes 5898244
  76.0 5.9 %collective-permute-start = (bf16[2,2,16,160]{3,2,1,0:T(8,128)(2,1)S(1)}, bf16[2,2,16,160]{3,2,1,0:T(8,128)(2,1)S(1)}, u32[]{:S(2)}, u32[]{:S(2)}) collective-permute-start(bf16[2,2,16,160]{3,2,1,0:T(8,128)(2,1)S(1)} %bitcast.215), channel_id=1, source_target_pairs={{0,8},{8,16},{16,24},{24,0},{1,9},{9,17},{17,25},{25,1},{2,10},{10... | collective-permute-start | bytes 61448 | tf_op jit(solution)/shard_map/ppermute | solution.py:177
  78.1 4.8 %collective-permute-start.1 = (bf16[2,2,16,160]{3,2,1,0:T(8,128)(2,1)S(1)}, bf16[2,2,16,160]{3,2,1,0:T(8,128)(2,1)S(1)}, u32[]{:S(2)}, u32[]{:S(2)}) collective-permute-start(bf16[2,2,16,160]{3,2,1,0:T(8,128)(2,1)S(1)} %bitcast.214), channel_id=1, source_target_pairs={{0,16},{8,24},{16,0},{24,8},{1,17},{9,25},{17,1},{25,9},{2,18},{10... | collective-permute-start | bytes 61448 | tf_op jit(solution)/shard_map/ppermute | solution.py:177
  80.4 3.9 %collective-permute-start.2 = (bf16[2,2,16,160]{3,2,1,0:T(8,128)(2,1)S(1)}, bf16[2,2,16,160]{3,2,1,0:T(8,128)(2,1)S(1)}, u32[]{:S(2)}, u32[]{:S(2)}) collective-permute-start(bf16[2,2,16,160]{3,2,1,0:T(8,128)(2,1)S(1)} %bitcast.213), channel_id=1, source_target_pairs={{0,24},{8,0},{16,8},{24,16},{1,25},{9,1},{17,9},{25,17},{2,26},{10... | collective-permute-start | bytes 61448 | tf_op jit(solution)/shard_map/ppermute | solution.py:177
